TPU v7x, 32 devices: a whole 2x2x4 slice. The times are simulated.
32 devices in a mesh: grp: 2 (over x), con: 16 (over z, y, core).
Axes of the slice: x: 2, y: 2, z: 4, core: 2. Of those that a mesh axis runs over, the one named last changes fastest.
Arguments:
- matrix: float32 [32768, 2048], P(('grp', 'con')), parts along dimension 0, may hold values from -0.046875 to 0.046875
- bounds_rhs: float32 [32768, 128], P(('grp', 'con')), parts along dimension 0, may hold values from -3 to 3
- costs: float32 [4096, 128], P(('grp', 'con')), parts along dimension 0, may hold values from -12 to 12
- upper: float32 [4096], P(('grp', 'con')), parts along dimension 0, may hold values from 0.5 to 2
- bound_mask: int32 [4096], P(('grp', 'con')), parts along dimension 0, may hold values 0 or 1
- node_map: int32 [3, 256], P(None, 'grp'), parts along dimension 1, may hold values from 0 to 63, as said below
- weights: int32 [256], P('grp'), parts along dimension 0, may hold values from 1 to 10
Outputs:
- primal: float32 [4096, 128], P(('grp', 'con')), parts along dimension 0
- dual: float32 [32768, 128], P(('grp', 'con')), parts along dimension 0
- multipliers: float32 [4096, 128], P(('grp', 'con')), parts along dimension 0
- gaps: float32 [4], P('grp'), parts along dimension 0
There are 2 independent parts, one for each index of `grp`. A program takes and returns all parts, laid end to end along the dimension named above; each array names one. Nothing has to cross between parts.
Inputs may be any that keep to these rules, and one draw needn't show every extreme that they name: `node_map`: row t numbers the 4 ** (t + 1) nodes of that section; each node holds 128 / 4 ** (t + 1) scenarios, and the nodes of row t + 1 split those of row t.
All inputs are finite; a program needn't handle non-finite values. No bound on the sum of `bound_mask` on one device may be relied on, other than what follows from the above.
Results may differ from a plain program's by a relative error of at most 0.0001.
Values sent between devices are 32-bit elements; how exact they have to be, the bound alone decides.
A program may use at most 64 MiB of HBM per device.

v0:
```python
import jax
import jax.numpy as jnp
from jax import lax
from jax.sharding import PartitionSpec as P

N = 2048
OUTER = 2
INNER = 2
highest = lax.Precision.HIGHEST
step_primal = 0.4
step_dual = 0.6
penalty = 1.0


def node_average(node_map, weights):
    weight_float = weights.astype(jnp.float32)
    probability = weight_float / jnp.sum(weight_float)
    same_node = (node_map[:, :, None] == node_map[:, None, :]).astype(jnp.float32)
    node_mass = same_node * probability[None, None, :]
    return (node_mass / jnp.sum(node_mass, axis=2, keepdims=True), probability)


def consensus(primal, averaging, column_index):
    averaged = jnp.einsum("tsr,jr->tjs", averaging, primal, precision=highest)
    section_of = column_index % (averaging.shape[0] + 1)
    section_hot = (
        section_of[None, :] == jnp.arange(averaging.shape[0], dtype=jnp.int32)[:, None]
    ).astype(jnp.float32)
    free_cols = 1.0 - jnp.sum(section_hot, axis=0)
    return jnp.sum(section_hot[:, :, None] * averaged, axis=0) + free_cols[:, None] * primal


def primal_step(primal, costs, multipliers, average, transposed, upper, flags, prox_weight):
    gradient = costs + multipliers + prox_weight * (primal - average) + transposed
    moved = jnp.maximum(primal - step_primal * gradient, 0.0)
    return jnp.where(flags[:, None] > 0, jnp.minimum(moved, upper[:, None]), moved)


def apply_rows(matrix, extrap):
    return jnp.dot(matrix, lax.all_gather(extrap, "con", axis=0, tiled=True), precision=highest)


def apply_columns(matrix, dual):
    return lax.psum_scatter(
        lax.dot_general(matrix, dual, (((0,), (0,)), ((), ())), precision=highest),
        "con",
        scatter_dimension=0,
        tiled=True,
    )


def body(matrix, bounds_rhs, costs, upper, bound_mask, node_map, weights):
    own_cols = costs.shape[0]
    scenario_count = costs.shape[1]
    averaging, probability = node_average(node_map, weights)
    start_col = lax.axis_index("con") * own_cols
    costs_all, upper_all, flags_all = (costs, upper, bound_mask.astype(jnp.float32))
    width = costs_all.shape[0]
    column_index = start_col + jnp.arange(width, dtype=jnp.int32)
    primal = jnp.zeros((width, scenario_count), jnp.float32)
    multipliers = jnp.zeros((width, scenario_count), jnp.float32)
    average = jnp.zeros((width, scenario_count), jnp.float32)
    transposed = jnp.zeros((width, scenario_count), jnp.float32)
    dual = jnp.zeros(bounds_rhs.shape, jnp.float32)
    partials = []
    for outer_turn in range(OUTER):
        prox_weight = 0.0 if outer_turn == 0 else penalty
        for inner_turn in range(INNER):
            moved = primal_step(
                primal,
                costs_all,
                multipliers,
                average,
                transposed,
                upper_all,
                flags_all,
                prox_weight,
            )
            extrap = 2.0 * moved - primal
            product = apply_rows(matrix, extrap)
            dual = jnp.maximum(dual + step_dual * (product - bounds_rhs), 0.0)
            primal = moved
            if outer_turn < OUTER - 1 or inner_turn < INNER - 1:
                transposed = apply_columns(matrix, dual)
        average = consensus(primal, averaging, column_index)
        deviation = primal - average
        multipliers = multipliers + penalty * deviation
        partial_value = jnp.sum(deviation * deviation * probability[None, :]) / N
        partial_value = lax.psum(partial_value, "con")
        partials.append(partial_value)
    gaps = jnp.stack(partials)
    return (primal, dual, multipliers, gaps)


def solution(mesh):
    placed = (
        P(("grp", "con"), None),
        P(("grp", "con"), None),
        P(("grp", "con"), None),
        P(("grp", "con")),
        P(("grp", "con")),
        P(None, "grp"),
        P("grp"),
    )
    return jax.shard_map(
        body,
        mesh=mesh,
        in_specs=placed,
        out_specs=(
            P(("grp", "con"), None),
            P(("grp", "con"), None),
            P(("grp", "con"), None),
            P("grp"),
        ),
        check_vma=False,
    )
```

profile of v0, /device:TPU:0, one launch (start us, length us, event | category | flops | bytes accessed | tf_op | source)
XLA Modules:
  0.0 413.3 jit_solution(4604648816111772595)
XLA Ops:
  7.2 0.0 all-gather.5.cloned.1.call-start
  7.2 0.7 convert_compare_fusion
  7.9 0.9 copy.23
  8.8 1.3 fusion.31
  10.1 0.0 all-gather.5.cloned.1.call-update
  10.1 0.0 reduce-scatter.4.cloned.1.call-start
  10.2 1.2 copy.25
  11.4 0.0 copy-start.2
  11.4 38.8 %all-gather.5.cloned.1.call-done = f32[2048,128]{0,1:T(8,128)} async-done(((f32[128,128]{0,1:T(8,128)}), f32[2048,128]{0,1:T(8,128)}) %all-gather.5.cloned.1.call-update) | async-done | bytes 1048592 | tf_op jit(solution)/shard_map/all_gather | solution.py:40
  50.3 0.0 copy-start
  50.3 12.0 %fusion.8 = f32[1024,128]{0,1:T(8,128)S(1)} fusion(f32[1024,128]{0,1:T(8,128)S(1)} %copy.25, f32[2048,128]{0,1:T(8,128)} %all-gather.5.cloned.1.call-done, f32[1024,2048]{1,0:T(8,128)} %param.7), kind=kOutput, calls=%fused_computation.15 | convolution fusion | flops 3221618688 | bytes 10485760 | tf_op jit(solution)/shard_map/dot_general | solution.py:40
  62.3 0.0 copy-done
  62.3 5.6 %convolution_bitcast_fusion.2 = f32[2048,128]{0,1:T(8,128)} fusion(f32[1024,128]{0,1:T(8,128)S(1)} %fusion.8, f32[1024,2048]{1,0:T(8,128)S(1)} %copy-done), kind=kOutput, calls=%fused_computation.2 | convolution fusion | flops 3221225472 | bytes 9961472 | tf_op jit(solution)/shard_map/dot_general | solution.py:45
  67.8 0.0 reduce-scatter.4.cloned.1.call-update
  67.9 0.0 all-gather.7.cloned.1.call-start
  67.9 57.0 %reduce-scatter.4.cloned.1.call-done = f32[128,128]{0,1:T(8,128)} async-done(((f32[2048,128]{0,1:T(8,128)}), f32[128,128]{0,1:T(8,128)}) %reduce-scatter.4.cloned.1.call-update) | async-done | bytes 65552 | tf_op jit(solution)/shard_map/reduce_scatter | solution.py:44
  124.9 0.0 copy-done.2
  124.9 1.5 multiply_subtract_fusion.2
  126.5 0.0 all-gather.7.cloned.1.call-update
  126.5 0.0 copy-start.3
  126.5 0.0 copy-start.1
  126.5 0.2 reduce-scatter.6.cloned.1.call-start
  126.7 37.0 %all-gather.7.cloned.1.call-done = f32[2048,128]{0,1:T(8,128)} async-done(((f32[128,128]{0,1:T(8,128)}), f32[2048,128]{0,1:T(8,128)}) %all-gather.7.cloned.1.call-update) | async-done | bytes 1048592 | tf_op jit(solution)/shard_map/all_gather | solution.py:40
  163.7 11.5 %fusion.10 = f32[1024,128]{0,1:T(8,128)S(1)} fusion(f32[1024,128]{0,1:T(8,128)S(1)} %fusion.8, f32[1024,128]{0,1:T(8,128)S(1)} %copy.25, f32[2048,128]{0,1:T(8,128)} %all-gather.7.cloned.1.call-done, f32[1024,2048]{1,0:T(8,128)} %param.7), kind=kOutput, calls=%fused_computation.17 | convolution fusion | flops 3221749760 | bytes 11010048 | tf_op jit(solution)/shard_map/dot_general | solution.py:40
  175.2 7.8 %convolution_bitcast_fusion.1 = f32[2048,128]{0,1:T(8,128)} fusion(f32[1024,128]{0,1:T(8,128)S(1)} %fusion.10, f32[1024,2048]{1,0:T(8,128)} %param.7), kind=kOutput, calls=%fused_computation.1 | convolution fusion | flops 3221225472 | bytes 9961472 | tf_op jit(solution)/shard_map/dot_general | solution.py:45
  183.0 0.0 reduce-scatter.6.cloned.1.call-update
  183.1 0.0 all-gather.9.cloned.1.call-start
  183.1 0.0 copy-done.3
  183.1 0.6 convert_reduce_fusion
  183.8 0.6 convert_divide_fusion
  184.4 0.0 copy-done.1
  184.4 0.2 select_reduce_fusion
  184.7 0.5 fusion.17
  185.2 0.1 copy.27
  185.3 54.8 %reduce-scatter.6.cloned.1.call-done = f32[128,128]{0,1:T(8,128)} async-done(((f32[2048,128]{0,1:T(8,128)}), f32[128,128]{0,1:T(8,128)}) %reduce-scatter.6.cloned.1.call-update) | async-done | bytes 65552 | tf_op jit(solution)/shard_map/reduce_scatter | solution.py:44
  240.1 1.5 multiply_subtract_fusion.1
  241.6 0.0 all-gather.9.cloned.1.call-update
  241.6 0.3 reduce-scatter.8.cloned.1.call-start
  241.9 36.7 %all-gather.9.cloned.1.call-done = f32[2048,128]{0,1:T(8,128)} async-done(((f32[128,128]{0,1:T(8,128)}), f32[2048,128]{0,1:T(8,128)}) %all-gather.9.cloned.1.call-update) | async-done | bytes 1048592 | tf_op jit(solution)/shard_map/all_gather | solution.py:40
  278.6 11.4 %fusion.12 = f32[1024,128]{0,1:T(8,128)S(1)} fusion(f32[1024,128]{0,1:T(8,128)S(1)} %fusion.10, f32[1024,128]{0,1:T(8,128)S(1)} %copy.25, f32[2048,128]{0,1:T(8,128)} %all-gather.9.cloned.1.call-done, f32[1024,2048]{1,0:T(8,128)} %param.7), kind=kOutput, calls=%fused_computation.19 | convolution fusion | flops 3221749760 | bytes 11010048 | tf_op jit(solution)/shard_map/dot_general | solution.py:40
  290.0 7.8 %convolution_bitcast_fusion = f32[2048,128]{0,1:T(8,128)} fusion(f32[1024,128]{0,1:T(8,128)S(1)} %fusion.12, f32[1024,2048]{1,0:T(8,128)} %param.7), kind=kOutput, calls=%fused_computation | convolution fusion | flops 3221225472 | bytes 9961472 | tf_op jit(solution)/shard_map/dot_general | solution.py:45
  297.9 0.0 reduce-scatter.8.cloned.1.call-update
  297.9 0.0 all-gather.11.cloned.1.call-start
  297.9 57.0 %reduce-scatter.8.cloned.1.call-done = f32[128,128]{0,1:T(8,128)} async-done(((f32[2048,128]{0,1:T(8,128)}), f32[128,128]{0,1:T(8,128)}) %reduce-scatter.8.cloned.1.call-update) | async-done | bytes 65552 | tf_op jit(solution)/shard_map/reduce_scatter | solution.py:44
  355.0 1.5 multiply_subtract_fusion
  356.5 0.0 all-gather.11.cloned.1.call-update
  356.5 0.5 fusion.18
  357.0 0.1 copy.33
  357.1 0.7 multiply_reduce_fusion.1
  359.1 31.6 %all-reduce = (f32[1]{0:T(128)}, f32[1]{0:T(128)}) all-reduce(f32[1]{0:T(128)} %bitcast.12, f32[1]{0:T(128)} %bitcast.11), channel_id=1, replica_groups=mesh['grp'=2,'con'=16] {'con'}, use_global_device_ids=true, to_apply=%region_11.12 | all-reduce | flops 2 | bytes 16 | tf_op jit(solution)/shard_map/psum | solution.py:89
  390.7 0.7 copy.34
  391.4 0.7 copy.36
  392.2 1.8 pad_maximum_fusion
  394.0 0.0 all-gather.11.cloned.1.call-done
  394.0 11.5 %fusion.14 = f32[1024,128]{0,1:T(8,128)S(1)} fusion(f32[1024,128]{0,1:T(8,128)S(1)} %fusion.12, f32[1024,128]{0,1:T(8,128)S(1)} %copy.25, f32[2048,128]{0,1:T(8,128)} %all-gather.11.cloned.1.call-done, f32[1024,2048]{1,0:T(8,128)} %param.7), kind=kOutput, calls=%fused_computation.21 | convolution fusion | flops 3221749760 | bytes 11010048 | tf_op jit(solution)/shard_map/dot_general | solution.py:40
  405.5 1.0 copy.35
  (4 shorter events, 0.0 us)
Async XLA Ops:
  7.2 43.1 %all-gather.5.cloned.1.call-start = ((), (), s32[]{:S(2)}) async-start(), calls=%async_computation.3 | async-start | bytes 1114112 | tf_op jit(solution)/shard_map/all_gather | solution.py:40
  10.1 114.8 %reduce-scatter.4.cloned.1.call-start = ((), (), s32[]{:S(2)}) async-start(), calls=%async_computation.4 | async-start | bytes 1114112 | tf_op jit(solution)/shard_map/reduce_scatter | solution.py:44
  11.4 113.5 %copy-start.2 = (f32[128]{0:T(128)S(1)}, f32[128]{0:T(128)}, u32[]{:S(2)}) copy-start(f32[128]{0:T(128)} %param.10) | copy-start | bytes 1540
  50.3 12.0 %copy-start = (f32[1024,2048]{1,0:T(8,128)S(1)}, f32[1024,2048]{1,0:T(8,128)}, u32[]{:S(2)}) copy-start(f32[1024,2048]{1,0:T(8,128)} %param.7) | copy-start | bytes 25165828
  67.9 95.9 %all-gather.7.cloned.1.call-start = ((), (), s32[]{:S(2)}) async-start(), calls=%async_computation.5 | async-start | bytes 1114112 | tf_op jit(solution)/shard_map/all_gather | solution.py:40
  126.5 56.7 %copy-start.3 = (s32[128]{0:T(128)S(1)}, s32[128]{0:T(128)}, u32[]{:S(2)}) copy-start(s32[128]{0:T(128)} %param.13) | copy-start | bytes 1540
  126.5 57.9 %copy-start.1 = (s32[3,128]{1,0:T(4,128)S(1)}, s32[3,128]{1,0:T(4,128)}, u32[]{:S(2)}) copy-start(s32[3,128]{1,0:T(4,128)} %param.12) | copy-start | bytes 4612
  126.5 113.6 %reduce-scatter.6.cloned.1.call-start = ((), (), s32[]{:S(2)}) async-start(), calls=%async_computation.6 | async-start | bytes 1114112 | tf_op jit(solution)/shard_map/reduce_scatter | solution.py:44
  183.1 95.5 %all-gather.9.cloned.1.call-start = ((), (), s32[]{:S(2)}) async-start(), calls=%async_computation.7 | async-start | bytes 1114112 | tf_op jit(solution)/shard_map/all_gather | solution.py:40
  241.6 113.4 %reduce-scatter.8.cloned.1.call-start = ((), (), s32[]{:S(2)}) async-start(), calls=%async_computation.8 | async-start | bytes 1114112 | tf_op jit(solution)/shard_map/reduce_scatter | solution.py:44
  297.9 96.1 %all-gather.11.cloned.1.call-start = ((), (), s32[]{:S(2)}) async-start(), calls=%async_computation.9 | async-start | bytes 1114112 | tf_op jit(solution)/shard_map/all_gather | solution.py:40
Sparse Core Ops, SparseCore 0:
  10.7 39.4 all-gather.4
  68.0 56.8 reduce-scatter.3
  127.9 35.7 all-gather.6
  183.2 56.8 reduce-scatter.5
  242.7 35.8 all-gather.8
  298.0 56.9 reduce-scatter.7
  357.9 35.7 all-gather.10
where the time goes:
time: 414 us; the launch traced here: 413 us
  waiting for transfers between devices  281 us (68%)
  matrix products  68.6 us (17%)
  blocking collectives  31.6 us (8%)
  between operations  15.6 us (4%)
  other arithmetic  10.5 us (3%)
  local copies, waits for them, and re-layouts  4.82 us (1%)
    reduce_scatter x3, waiting for transfers between devices, apply_columns(): lax.psum_scatter(lax.dot_general(matrix, dual, (((0,), (0,)), ((), ())),...  169 us
    all_gather x4, waiting for transfers between devices, apply_rows(): lax.all_gather(extrap, 'con', axis=0, tiled=True)  112 us
    dot_general x4, matrix products, apply_rows(): jnp.dot(matrix, lax.all_gather(extrap, 'con', axis=0, tiled=True), precis...  46.3 us
    psum x1, blocking collectives, body(): partial_value = lax.psum(partial_value, 'con')  31.6 us
    dot_general x3, matrix products, apply_columns(): lax.dot_general(matrix, dual, (((0,), (0,)), ((), ())), precision=highest)  21.3 us
  transfers between devices with their start and end apart: 7, of which 6 were waited for; matrix products, arithmetic and copies ran while one was open for 2% of the time, Pallas kernels for 0%

commit v1 on v0

--- a/solution.py
+++ b/solution.py
@@ -86,7 +86,11 @@
         deviation = primal - average
         multipliers = multipliers + penalty * deviation
         partial_value = jnp.sum(deviation * deviation * probability[None, :]) / N
-        partial_value = lax.psum(partial_value, "con")
+        partial_value = partial_value
+        for hop in (1, 2, 4, 8):
+            partial_value = partial_value + lax.ppermute(
+                partial_value, "con", [(dev, dev ^ hop) for dev in range(16)]
+            )
         partials.append(partial_value)
     gaps = jnp.stack(partials)
     return (primal, dual, multipliers, gaps)

time: 414 us -> 413 us (level)
  blocking collectives: 31.6 us -> 0 us
  starting transfers between devices: 0.69 us -> 18.1 us
  waiting for transfers between devices: 281 us -> 292 us
  between operations: 15.6 us -> 20.6 us
    psum x1 -> x0, blocking collectives: 31.6 us -> none  [body(): partial_value = lax.psum(partial_value, 'con')]
    ppermute x0 -> x8, starting transfers between devices: none -> 17.4 us  [body(): lax.ppermute(partial_value, 'con', [(dev, dev ^ hop) for dev in range(16)])]
    all_gather x4, waiting for transfers between devices: 112 us -> 122 us  [apply_rows(): lax.all_gather(extrap, 'con', axis=0, tiled=True)]
  transfers between devices with their start and end apart: 7 -> 15, of which waited for: 6 -> 8; matrix products, arithmetic and copies ran while one was open for 2% -> 2% of each run, Pallas kernels for 0% -> 0%
where the time goes in v1:
time: 413 us
  waiting for transfers between devices  292 us (71%)
  matrix products  68.6 us (17%)
  between operations  20.6 us (5%)
  starting transfers between devices  18.1 us (4%)
  other arithmetic  9.27 us (2%)
  local copies, waits for them, and re-layouts  4.82 us (1%)
    reduce_scatter x3, waiting for transfers between devices, apply_columns(): lax.psum_scatter(lax.dot_general(matrix, dual, (((0,), (0,)), ((), ())),...  169 us
    all_gather x4, waiting for transfers between devices, apply_rows(): lax.all_gather(extrap, 'con', axis=0, tiled=True)  122 us
    dot_general x4, matrix products, apply_rows(): jnp.dot(matrix, lax.all_gather(extrap, 'con', axis=0, tiled=True), precis...  46.4 us
    dot_general x3, matrix products, apply_columns(): lax.dot_general(matrix, dual, (((0,), (0,)), ((), ())), precision=highest)  21.2 us
    ppermute x8, starting transfers between devices, body(): lax.ppermute(partial_value, 'con', [(dev, dev ^ hop) for dev in range(16)])  17.4 us
  transfers between devices with their start and end apart: 15, of which 8 were waited for; matrix products, arithmetic and copies ran while one was open for 2% of the time, Pallas kernels for 0%

profile of v1, /device:TPU:0, one launch (start us, length us, event | category | flops | bytes accessed | tf_op | source)
XLA Modules:
  0.0 413.0 jit_solution(10648010877519822180)
XLA Ops:
  7.2 0.0 all-gather.5.cloned.1.call-start
  7.2 0.7 convert_compare_fusion
  7.9 0.9 copy.23
  8.8 1.3 fusion.31
  10.1 0.0 all-gather.5.cloned.1.call-update
  10.1 0.0 reduce-scatter.4.cloned.1.call-start
  10.2 1.2 copy.25
  11.4 0.0 copy-start.2
  11.4 38.8 %all-gather.5.cloned.1.call-done = f32[2048,128]{0,1:T(8,128)} async-done(((f32[128,128]{0,1:T(8,128)}), f32[2048,128]{0,1:T(8,128)}) %all-gather.5.cloned.1.call-update) | async-done | bytes 1048592 | tf_op jit(solution)/shard_map/all_gather | solution.py:40
  50.3 0.0 copy-start
  50.3 12.0 %fusion.8 = f32[1024,128]{0,1:T(8,128)S(1)} fusion(f32[1024,128]{0,1:T(8,128)S(1)} %copy.25, f32[2048,128]{0,1:T(8,128)} %all-gather.5.cloned.1.call-done, f32[1024,2048]{1,0:T(8,128)} %param.7), kind=kOutput, calls=%fused_computation.15 | convolution fusion | flops 3221618688 | bytes 10485760 | tf_op jit(solution)/shard_map/dot_general | solution.py:40
  62.3 0.0 copy-done
  62.3 5.5 %convolution_bitcast_fusion.2 = f32[2048,128]{0,1:T(8,128)} fusion(f32[1024,128]{0,1:T(8,128)S(1)} %fusion.8, f32[1024,2048]{1,0:T(8,128)S(1)} %copy-done), kind=kOutput, calls=%fused_computation.2 | convolution fusion | flops 3221225472 | bytes 9961472 | tf_op jit(solution)/shard_map/dot_general | solution.py:45
  67.8 0.0 reduce-scatter.4.cloned.1.call-update
  67.9 0.0 all-gather.7.cloned.1.call-start
  67.9 57.0 %reduce-scatter.4.cloned.1.call-done = f32[128,128]{0,1:T(8,128)} async-done(((f32[2048,128]{0,1:T(8,128)}), f32[128,128]{0,1:T(8,128)}) %reduce-scatter.4.cloned.1.call-update) | async-done | bytes 65552 | tf_op jit(solution)/shard_map/reduce_scatter | solution.py:44
  125.0 0.0 copy-done.2
  125.0 1.5 multiply_subtract_fusion.2
  126.5 0.0 all-gather.7.cloned.1.call-update
  126.5 0.0 copy-start.3
  126.5 0.0 copy-start.1
  126.5 0.2 reduce-scatter.6.cloned.1.call-start
  126.7 37.0 %all-gather.7.cloned.1.call-done = f32[2048,128]{0,1:T(8,128)} async-done(((f32[128,128]{0,1:T(8,128)}), f32[2048,128]{0,1:T(8,128)}) %all-gather.7.cloned.1.call-update) | async-done | bytes 1048592 | tf_op jit(solution)/shard_map/all_gather | solution.py:40
  163.8 11.5 %fusion.10 = f32[1024,128]{0,1:T(8,128)S(1)} fusion(f32[1024,128]{0,1:T(8,128)S(1)} %fusion.8, f32[1024,128]{0,1:T(8,128)S(1)} %copy.25, f32[2048,128]{0,1:T(8,128)} %all-gather.7.cloned.1.call-done, f32[1024,2048]{1,0:T(8,128)} %param.7), kind=kOutput, calls=%fused_computation.17 | convolution fusion | flops 3221749760 | bytes 11010048 | tf_op jit(solution)/shard_map/dot_general | solution.py:40
  175.2 7.8 %convolution_bitcast_fusion.1 = f32[2048,128]{0,1:T(8,128)} fusion(f32[1024,128]{0,1:T(8,128)S(1)} %fusion.10, f32[1024,2048]{1,0:T(8,128)} %param.7), kind=kOutput, calls=%fused_computation.1 | convolution fusion | flops 3221225472 | bytes 9961472 | tf_op jit(solution)/shard_map/dot_general | solution.py:45
  183.0 0.0 reduce-scatter.6.cloned.1.call-update
  183.1 0.0 all-gather.9.cloned.1.call-start
  183.1 0.0 copy-done.3
  183.1 0.6 convert_reduce_fusion
  183.8 0.6 convert_divide_fusion
  184.4 0.0 copy-done.1
  184.4 0.2 select_reduce_fusion
  184.7 0.5 fusion.17
  185.2 0.1 copy.27
  185.3 54.8 %reduce-scatter.6.cloned.1.call-done = f32[128,128]{0,1:T(8,128)} async-done(((f32[2048,128]{0,1:T(8,128)}), f32[128,128]{0,1:T(8,128)}) %reduce-scatter.6.cloned.1.call-update) | async-done | bytes 65552 | tf_op jit(solution)/shard_map/reduce_scatter | solution.py:44
  240.1 1.5 multiply_subtract_fusion.1
  241.6 0.0 all-gather.9.cloned.1.call-update
  241.7 0.3 reduce-scatter.8.cloned.1.call-start
  241.9 36.6 %all-gather.9.cloned.1.call-done = f32[2048,128]{0,1:T(8,128)} async-done(((f32[128,128]{0,1:T(8,128)}), f32[2048,128]{0,1:T(8,128)}) %all-gather.9.cloned.1.call-update) | async-done | bytes 1048592 | tf_op jit(solution)/shard_map/all_gather | solution.py:40
  278.5 11.5 %fusion.12 = f32[1024,128]{0,1:T(8,128)S(1)} fusion(f32[1024,128]{0,1:T(8,128)S(1)} %fusion.10, f32[1024,128]{0,1:T(8,128)S(1)} %copy.25, f32[2048,128]{0,1:T(8,128)} %all-gather.9.cloned.1.call-done, f32[1024,2048]{1,0:T(8,128)} %param.7), kind=kOutput, calls=%fused_computation.19 | convolution fusion | flops 3221749760 | bytes 11010048 | tf_op jit(solution)/shard_map/dot_general | solution.py:40
  290.0 7.8 %convolution_bitcast_fusion = f32[2048,128]{0,1:T(8,128)} fusion(f32[1024,128]{0,1:T(8,128)S(1)} %fusion.12, f32[1024,2048]{1,0:T(8,128)} %param.7), kind=kOutput, calls=%fused_computation | convolution fusion | flops 3221225472 | bytes 9961472 | tf_op jit(solution)/shard_map/dot_general | solution.py:45
  297.8 0.0 reduce-scatter.8.cloned.1.call-update
  297.8 0.0 all-gather.11.cloned.1.call-start
  297.9 57.0 %reduce-scatter.8.cloned.1.call-done = f32[128,128]{0,1:T(8,128)} async-done(((f32[2048,128]{0,1:T(8,128)}), f32[128,128]{0,1:T(8,128)}) %reduce-scatter.8.cloned.1.call-update) | async-done | bytes 65552 | tf_op jit(solution)/shard_map/reduce_scatter | solution.py:44
  354.9 1.5 multiply_subtract_fusion
  356.4 0.0 all-gather.11.cloned.1.call-update
  356.4 0.7 copy.34
  357.2 0.5 fusion.18
  357.7 0.1 copy.33
  357.8 0.7 multiply_reduce_fusion.1
  359.8 0.7 copy.36
  360.5 0.8 collective-permute-start
  361.3 1.5 collective-permute-start.4
  363.4 2.6 collective-permute-start.1
  366.7 2.1 collective-permute-start.5
  369.4 2.7 collective-permute-start.2
  372.7 2.1 collective-permute-start.6
  375.4 2.7 collective-permute-start.3
  378.8 2.9 collective-permute-start.7
  382.3 0.9 collective-permute-done.7
  383.9 0.6 pad_maximum_fusion
  384.4 9.2 %all-gather.11.cloned.1.call-done = f32[2048,128]{0,1:T(8,128)} async-done(((f32[128,128]{0,1:T(8,128)}), f32[2048,128]{0,1:T(8,128)}) %all-gather.11.cloned.1.call-update) | async-done | bytes 1048592 | tf_op jit(solution)/shard_map/all_gather | solution.py:40
  393.7 11.5 %fusion.14 = f32[1024,128]{0,1:T(8,128)S(1)} fusion(f32[1024,128]{0,1:T(8,128)S(1)} %fusion.12, f32[1024,128]{0,1:T(8,128)S(1)} %copy.25, f32[2048,128]{0,1:T(8,128)} %all-gather.11.cloned.1.call-done, f32[1024,2048]{1,0:T(8,128)} %param.7), kind=kOutput, calls=%fused_computation.21 | convolution fusion | flops 3221749760 | bytes 11010048 | tf_op jit(solution)/shard_map/dot_general | solution.py:40
  405.1 1.0 copy.35
  (11 shorter events, 0.0 us)
Async XLA Ops:
  7.2 43.1 %all-gather.5.cloned.1.call-start = ((), (), s32[]{:S(2)}) async-start(), calls=%async_computation.3 | async-start | bytes 1114112 | tf_op jit(solution)/shard_map/all_gather | solution.py:40
  10.1 114.8 %reduce-scatter.4.cloned.1.call-start = ((), (), s32[]{:S(2)}) async-start(), calls=%async_computation.4 | async-start | bytes 1114112 | tf_op jit(solution)/shard_map/reduce_scatter | solution.py:44
  11.4 113.5 %copy-start.2 = (f32[128]{0:T(128)S(1)}, f32[128]{0:T(128)}, u32[]{:S(2)}) copy-start(f32[128]{0:T(128)} %param.10) | copy-start | bytes 1540
  50.3 12.0 %copy-start = (f32[1024,2048]{1,0:T(8,128)S(1)}, f32[1024,2048]{1,0:T(8,128)}, u32[]{:S(2)}) copy-start(f32[1024,2048]{1,0:T(8,128)} %param.7) | copy-start | bytes 25165828
  67.9 95.9 %all-gather.7.cloned.1.call-start = ((), (), s32[]{:S(2)}) async-start(), calls=%async_computation.5 | async-start | bytes 1114112 | tf_op jit(solution)/shard_map/all_gather | solution.py:40
  126.5 56.7 %copy-start.3 = (s32[128]{0:T(128)S(1)}, s32[128]{0:T(128)}, u32[]{:S(2)}) copy-start(s32[128]{0:T(128)} %param.13) | copy-start | bytes 1540
  126.5 57.9 %copy-start.1 = (s32[3,128]{1,0:T(4,128)S(1)}, s32[3,128]{1,0:T(4,128)}, u32[]{:S(2)}) copy-start(s32[3,128]{1,0:T(4,128)} %param.12) | copy-start | bytes 4612
  126.5 113.6 %reduce-scatter.6.cloned.1.call-start = ((), (), s32[]{:S(2)}) async-start(), calls=%async_computation.6 | async-start | bytes 1114112 | tf_op jit(solution)/shard_map/reduce_scatter | solution.py:44
  183.1 95.5 %all-gather.9.cloned.1.call-start = ((), (), s32[]{:S(2)}) async-start(), calls=%async_computation.7 | async-start | bytes 1114112 | tf_op jit(solution)/shard_map/all_gather | solution.py:40
  241.7 113.2 %reduce-scatter.8.cloned.1.call-start = ((), (), s32[]{:S(2)}) async-start(), calls=%async_computation.8 | async-start | bytes 1114112 | tf_op jit(solution)/shard_map/reduce_scatter | solution.py:44
  297.8 95.8 %all-gather.11.cloned.1.call-start = ((), (), s32[]{:S(2)}) async-start(), calls=%async_computation.9 | async-start | bytes 1114112 | tf_op jit(solution)/shard_map/all_gather | solution.py:40
  360.5 2.3 collective-permute-start
  361.3 4.7 %collective-permute-start.4 = (f32[]{:T(128)}, f32[]{:T(128)}, u32[]{:S(2)}, u32[]{:S(2)}) collective-permute-start(f32[]{:T(128)} %div.25), channel_id=1, source_target_pairs={{0,1},{1,0},{2,3},{3,2},{4,5},{5,4},{6,7},{7,6},{8,9},{9,8},{10,11... | collective-permute-start | bytes 20 | tf_op jit(solution)/shard_map/ppermute | solution.py:91
  363.4 5.4 %collective-permute-start.1 = (f32[]{:T(128)}, f32[]{:T(128)}, u32[]{:S(2)}, u32[]{:S(2)}) collective-permute-start(f32[]{:T(128)} %add.108), channel_id=1, source_target_pairs={{0,2},{1,3},{2,0},{3,1},{4,6},{5,7},{6,4},{7,5},{8,10},{9,11},{10,... | collective-permute-start | bytes 20 | tf_op jit(solution)/shard_map/ppermute | solution.py:91
  366.7 5.4 %collective-permute-start.5 = (f32[]{:T(128)}, f32[]{:T(128)}, u32[]{:S(2)}, u32[]{:S(2)}) collective-permute-start(f32[]{:T(128)} %add.112), channel_id=1, source_target_pairs={{0,2},{1,3},{2,0},{3,1},{4,6},{5,7},{6,4},{7,5},{8,10},{9,11},{10,... | collective-permute-start | bytes 20 | tf_op jit(solution)/shard_map/ppermute | solution.py:91
  369.4 5.4 %collective-permute-start.2 = (f32[]{:T(128)}, f32[]{:T(128)}, u32[]{:S(2)}, u32[]{:S(2)}) collective-permute-start(f32[]{:T(128)} %add.109), channel_id=1, source_target_pairs={{0,4},{1,5},{2,6},{3,7},{4,0},{5,1},{6,2},{7,3},{8,12},{9,13},{10,... | collective-permute-start | bytes 20 | tf_op jit(solution)/shard_map/ppermute | solution.py:91
  372.7 5.5 %collective-permute-start.6 = (f32[]{:T(128)}, f32[]{:T(128)}, u32[]{:S(2)}, u32[]{:S(2)}) collective-permute-start(f32[]{:T(128)} %add.113), channel_id=1, source_target_pairs={{0,4},{1,5},{2,6},{3,7},{4,0},{5,1},{6,2},{7,3},{8,12},{9,13},{10,... | collective-permute-start | bytes 20 | tf_op jit(solution)/shard_map/ppermute | solution.py:91
  375.4 6.3 %collective-permute-start.3 = (f32[]{:T(128)}, f32[]{:T(128)}, u32[]{:S(2)}, u32[]{:S(2)}) collective-permute-start(f32[]{:T(128)} %add.110), channel_id=1, source_target_pairs={{0,8},{1,9},{2,10},{3,11},{4,12},{5,13},{6,14},{7,15},{8,0},{9,1},... | collective-permute-start | bytes 20 | tf_op jit(solution)/shard_map/ppermute | solution.py:91
  378.8 4.5 %collective-permute-start.7 = (f32[]{:T(128)}, f32[]{:T(128)}, u32[]{:S(2)}, u32[]{:S(2)}) collective-permute-start(f32[]{:T(128)} %add.114), channel_id=1, source_target_pairs={{0,8},{1,9},{2,10},{3,11},{4,12},{5,13},{6,14},{7,15},{8,0},{9,1},... | collective-permute-start | bytes 20 | tf_op jit(solution)/shard_map/ppermute | solution.py:91
Sparse Core Ops, SparseCore 0:
  10.7 39.4 all-gather.4
  68.0 56.9 reduce-scatter.3
  127.9 35.7 all-gather.6
  183.2 56.9 reduce-scatter.5
  242.7 35.7 all-gather.8
  298.0 56.8 reduce-scatter.7
  357.9 35.7 all-gather.10
